TPU v7x, 32 devices: a whole 2x2x4 slice. The times are simulated.
32 devices in a mesh: shard: 32 (over z, y, x, core).
Axes of the slice: x: 2, y: 2, z: 4, core: 2. Of those that a mesh axis runs over, the one named last changes fastest.
Arguments:
- hidden: bfloat16 [96, 512, 768], P('shard'), may hold values from -6 to 6
- teacher_input: bfloat16 [96, 512, 768], P('shard'), may hold values from -6 to 6
- cotangent: bfloat16 [96, 512, 768], P('shard'), may hold values from -6 to 6
- lengths: int32 [96], P('shard'), may hold values from 33 to 512, as said below
- lat_qkv: float32 [768, 2304], P('shard'), as said below
- lat_out: float32 [768, 768], P('shard'), as said below
- lat_up: float32 [768, 3072], P('shard'), as said below
- lat_down: float32 [3072, 768], P('shard'), as said below
- bias_q: float32 [768], replicated, may hold values from -0.5 to 0.5
- bias_v: float32 [768], replicated, may hold values from -0.5 to 0.5
- bias_out: float32 [768], replicated, may hold values from -0.5 to 0.5
- bias_up: float32 [3072], replicated, may hold values from -0.5 to 0.5
- bias_down: float32 [768], replicated, may hold values from -0.5 to 0.5
- gain_one: float32 [768], replicated, may hold values from 0.5 to 1.5
- shift_one: float32 [768], replicated, may hold values from -0.3 to 0.3
- gain_two: float32 [768], replicated, may hold values from 0.5 to 1.5
- shift_two: float32 [768], replicated, may hold values from -0.3 to 0.3
- clips: float32 [4], replicated, as said below
- teach_qkv: bfloat16 [768, 2304], P('shard'), may hold values from -0.21875 to 0.21875
- teach_out: bfloat16 [768, 768], P('shard'), may hold values from -1.75 to 1.75
- teach_up: bfloat16 [768, 3072], P('shard'), may hold values from -0.21875 to 0.21875
- teach_down: bfloat16 [3072, 768], P('shard'), may hold values from -0.109375 to 0.109375
Outputs:
- mixed_out: bfloat16 [96, 512, 768], P('shard')
- input_grad: bfloat16 [96, 512, 768], P('shard')
- grad_lat_qkv: float32 [768, 2304], P('shard')
- grad_lat_out: float32 [768, 768], P('shard')
- grad_lat_up: float32 [768, 3072], P('shard')
- grad_lat_down: float32 [3072, 768], P('shard')
- grad_bias_q: float32 [768], replicated
- grad_bias_v: float32 [768], replicated
- grad_bias_out: float32 [768], replicated
- grad_bias_up: float32 [3072], replicated
- grad_bias_down: float32 [768], replicated
- grad_gain_one: float32 [768], replicated
- grad_shift_one: float32 [768], replicated
- grad_gain_two: float32 [768], replicated
- grad_shift_two: float32 [768], replicated
- grad_clips: float32 [4], replicated
Inputs may be any that keep to these rules, and one draw needn't show every extreme that they name: `lengths`: live tokens of each row, at the start of the row; some row has all 512. `lat_qkv`: no entry is zero; within each matrix every magnitude lies within a factor of ten of the largest. `lat_out`: no entry is zero; within each matrix every magnitude lies within a factor of ten of the largest. `lat_up`: no entry is zero; within each matrix every magnitude lies within a factor of ten of the largest. `lat_down`: no entry is zero; within each matrix every magnitude lies within a factor of ten of the largest. `clips`: all four bounds are positive.
All inputs are finite; a program needn't handle non-finite values.
Results may differ from a plain program's by a relative error of at most 0.015.
The roundings to bfloat16 on the way count: a program that leaves them out, or rounds other values in their place, can miss the bound.
Values may be sent and summed in bfloat16 or wider, within the bound.
A program may use at most 320 MiB of HBM per device.

v0:
```python
import functools
import math

import jax
import jax.numpy as jnp
from jax import lax
from jax.experimental import pallas as pl
from jax.experimental.pallas import tpu as pltpu
from jax.sharding import PartitionSpec as P

D = 768
FF = 3072
HEAD_DIM = 64
PAIR = 2 * HEAD_DIM
PAIRS = D // PAIR
DOUBLE, TRIPLE = 2 * PAIR, 3 * PAIR
CHUNKS = FF // D

EPSILON = 1e-05
MASKED = -1000000000.0
SCALE = 1.0 / math.sqrt(HEAD_DIM)

F32 = jnp.float32
BF16 = jnp.bfloat16
MESH = pl.DeviceIdType.MESH
VMEM_LIMIT = 63 * 1024 * 1024


def nn(left, right):
    return lax.dot_general(left, right, (((1,), (0,)), ((), ())), preferred_element_type=F32)


def nt(left, right):
    return lax.dot_general(left, right, (((1,), (1,)), ((), ())), preferred_element_type=F32)


def tn(left, right):
    return lax.dot_general(left, right, (((0,), (0,)), ((), ())), preferred_element_type=F32)


def signed_mean(latent):
    factor = jnp.mean(jnp.abs(latent), axis=1, keepdims=True)
    sign = jnp.where(latent > 0, 1.0, jnp.where(latent < 0, -1.0, 0.0))
    return (factor * sign).astype(BF16)


def normalize(value):
    center = value - jnp.mean(value, axis=-1, keepdims=True)
    inverse = lax.rsqrt(jnp.mean(center * center, axis=-1, keepdims=True) + EPSILON)
    return center * inverse, inverse


def norm_back(d_normed, normed, inverse):
    first = jnp.mean(d_normed, axis=-1, keepdims=True)
    second = jnp.mean(d_normed * normed, axis=-1, keepdims=True)
    return inverse * (d_normed - first - normed * second)


def normal_cdf(value):
    return 0.5 * (1.0 + lax.erf(value * (1.0 / math.sqrt(2.0))))


def column_sum(value):
    return jnp.sum(value, axis=0, keepdims=True)


def head_halves(pair):
    first = lax.broadcasted_iota(jnp.int32, pair.shape, 1) < HEAD_DIM
    zero = jnp.zeros_like(pair)
    return jnp.where(first, pair, zero), jnp.where(first, zero, pair)


def mask_columns(tokens, length):
    shape = (tokens, PAIR)
    first = lax.broadcasted_iota(jnp.int32, shape, 1) == 0
    dead = jnp.logical_and(first, lax.broadcasted_iota(jnp.int32, shape, 0) >= length)
    return jnp.where(dead, MASKED, 0.0).astype(BF16), jnp.where(first, 1.0, 0.0).astype(BF16)


def attend_pair(queries, keys, values, length):
    values_t = values.T
    beside_keys, beside_queries = mask_columns(queries.shape[0], length)
    wide_keys = jnp.concatenate([keys, beside_keys], axis=1)
    contexts, log_totals = [], []
    for head, one in enumerate(head_halves(queries)):
        masked = nt(wide_keys, jnp.concatenate([one, beside_queries], axis=1))
        top = jnp.max(masked, axis=0, keepdims=True)
        expo = jnp.exp(masked - top)
        total = jnp.sum(expo, axis=0, keepdims=True)
        probs = (expo * (1.0 / total)).astype(BF16)
        contexts.append(nn(values_t[HEAD_DIM * head : HEAD_DIM * (head + 1)], probs))
        log_totals.append(top + jnp.log(total))
    return jnp.concatenate(contexts, axis=0).T, jnp.concatenate(log_totals, axis=0)


def attend_pair_back(queries, keys, values, t_queries, t_keys, log_totals, row_dots, d_context, length):
    tokens = queries.shape[0]
    beside_keys, beside_queries = mask_columns(tokens, length)
    wide_keys = jnp.concatenate([keys, beside_keys], axis=1)
    live = lax.broadcasted_iota(jnp.int32, (tokens, DOUBLE), 0) < length
    both_keys = jnp.where(live, jnp.concatenate([keys, -t_keys], axis=1), 0.0).astype(BF16)
    share = jnp.where(live, 1.0 / tokens, 0.0).astype(BF16)
    keys_t = keys.T
    d_queries, d_keys, d_values = [], [], []
    heads = zip(head_halves(queries), head_halves(d_context), head_halves(t_queries))
    for head, (one, d_one, t_one) in enumerate(heads):
        masked = nt(wide_keys, jnp.concatenate([one, beside_queries], axis=1))
        extra = nt(both_keys, jnp.concatenate([one, t_one], axis=1) * share)
        probs = jnp.exp(masked - log_totals[head : head + 1])
        d_probs = nt(values, d_one)
        d_values.append(nn(probs.astype(BF16), d_one))
        d_scores = (probs * (d_probs - row_dots[head : head + 1]) + extra).astype(BF16)
        d_keys.append(nn(d_scores, one))
        d_queries.append(nn(keys_t[HEAD_DIM * head : HEAD_DIM * (head + 1)], d_scores))
    d_q = (jnp.concatenate(d_queries, axis=0).T * SCALE).astype(BF16)
    return d_q, (d_keys[0] + d_keys[1]).astype(BF16), (d_values[0] + d_values[1]).astype(BF16)


def pair_columns(pair, width=PAIR):
    return pl.ds(pl.multiple_of(pair * width, PAIR), width)


def by_pairs(matrix):
    split = matrix.reshape(matrix.shape[0], 3, PAIRS, PAIR)
    return split.transpose(0, 2, 1, 3).reshape(matrix.shape[0], 3 * D)


def by_kinds(matrix):
    split = matrix.reshape(matrix.shape[0], PAIRS, 3, PAIR)
    return split.transpose(0, 2, 1, 3).reshape(matrix.shape[0], 3 * D)


def teacher_pair(pair, x, length, w_qkv, tqk_ref, context_ref):
    joined = nn(x, w_qkv[:, pair_columns(pair, TRIPLE)]).astype(BF16)
    queries, keys, values = (joined[:, PAIR * i : PAIR * (i + 1)] for i in range(3))
    queries = (queries.astype(F32) * SCALE).astype(BF16)
    tqk_ref[:, pair_columns(pair, DOUBLE)] = jnp.concatenate([queries, keys], axis=1)
    mixed, _ = attend_pair(queries, keys, values, length)
    context_ref[:, pair_columns(pair)] = mixed.astype(BF16)


def teacher_last(x, context, w_out, w_up, w_down, between):
    first, _ = normalize(x.astype(F32) + nn(context, w_out[...]))
    first_low = first.astype(BF16)
    total = first
    for c in range(CHUNKS):
        between(c)
        inner = nn(first_low, w_up[:, D * c : D * (c + 1)])
        total = total + nn((inner * normal_cdf(inner)).astype(BF16), w_down[D * c : D * (c + 1), :])
    return normalize(total)[0]


def student_pair(pair, a_in, length, w_qkv, bias_q, bias_v, qkv_ref, context_ref, log_ref):
    joined = nn(a_in, w_qkv[:, pair_columns(pair, TRIPLE)])
    queries = (joined[:, :PAIR] + bias_q[:, pair_columns(pair)]).astype(BF16)
    queries = (queries.astype(F32) * SCALE).astype(BF16)
    keys = joined[:, PAIR:DOUBLE].astype(BF16)
    values = (joined[:, DOUBLE:] + bias_v[:, pair_columns(pair)]).astype(BF16)
    qkv_ref[:, pair_columns(pair, TRIPLE)] = jnp.concatenate([queries, keys, values], axis=1)
    mixed, log_totals = attend_pair(queries, keys, values, length)
    context_ref[:, pair_columns(pair)] = mixed
    log_ref[pair] = log_totals


def teacher_kernel(lengths, x_ref, w_qkv, w_out, w_up, w_down, tqk_ref, final_ref, context):
    length = lengths[pl.program_id(0)]

    @pl.loop(0, PAIRS)
    def _(pair):
        teacher_pair(pair, x_ref[0], length, w_qkv, tqk_ref.at[0], context)

    final_ref[0] = teacher_last(x_ref[0], context[...], w_out, w_up, w_down, lambda c: None)


def student_attend_kernel(lengths, clips, x_ref, w_qkv, bias_q, bias_v, qkv_ref, context_ref, log_ref, a_in):
    length = lengths[pl.program_id(0)]
    a_in[...] = jnp.clip(x_ref[0].astype(F32), -clips[0], clips[0]).astype(BF16)

    @pl.loop(0, PAIRS)
    def _(pair):
        student_pair(
            pair, a_in[...], length, w_qkv, bias_q, bias_v, qkv_ref.at[0], context_ref.at[0], log_ref.at[0]
        )


(S_OUT, S_UP, S_DOWN, S_GAIN_ONE, S_SHIFT_ONE, S_GAIN_TWO, S_SHIFT_TWO, S_CLIP_ONE, S_CLIP_TWO, S_CLIP_THREE) = (
    0, 1, 5, 6, 7, 8, 9, 10, 11, 12,
)
S_ROWS = 16
(Q_QUERY, Q_VALUE, Q_CLIP) = (0, 1, 2)
Q_ROWS = 8
ABOVE, BELOW = 4.0, -4.0


def student_middle_kernel(
    lengths, clips, x_ref, cotangent_ref, final_ref, context_ref, w_out, w_up, w_down,
    bias_out, bias_up, bias_down, gain_one, shift_one, gain_two, shift_two,
    mixed_ref, act_ref, d_pre_ref, up_in_ref, d_down_ref, cut_ref, d_attn_ref, d_res_ref, d_context_ref, dots_ref,
    sums_ref, slope,
):
    block = x_ref.shape[1]
    row, part = pl.program_id(0), pl.program_id(1)
    length = lengths[row] - part * block

    @pl.when(jnp.logical_and(row == 0, part == 0))
    def _():
        sums_ref[...] = jnp.zeros_like(sums_ref)

    def add(at, value):
        sums_ref[at : at + 1] += value

    def vector(ref):
        return ref[...].reshape(1, ref.shape[0])

    cut = jnp.clip(context_ref[0], -clips[1], clips[1]).astype(BF16)
    cut_ref[0] = cut
    normed_one, inverse_one = normalize(x_ref[0].astype(F32) + nn(cut, w_out[...]) + vector(bias_out))
    h_one = normed_one * vector(gain_one) + vector(shift_one)
    up_in = jnp.clip(h_one, -clips[2], clips[2]).astype(BF16)
    up_in_ref[0] = up_in
    total = h_one + vector(bias_down)
    for c in range(CHUNKS):
        columns = slice(D * c, D * (c + 1))
        pre = nn(up_in, w_up[:, columns]) + vector(bias_up)[:, columns]
        cdf = normal_cdf(pre)
        value = pre * cdf
        rise = cdf + pre * jnp.exp(-0.5 * pre * pre) * (1.0 / math.sqrt(2.0 * math.pi))
        rise = jnp.where(value > clips[3], ABOVE, jnp.where(value < -clips[3], BELOW, rise))
        slope[:, columns] = rise
        act = jnp.clip(value, -clips[3], clips[3]).astype(BF16)
        act_ref[0, :, columns] = act
        total = total + nn(act, w_down[columns, :])
    normed_two, inverse_two = normalize(total)
    out = normed_two * vector(gain_two) + vector(shift_two)
    mixed_ref[0] = out.astype(BF16)
    live = lax.broadcasted_iota(jnp.int32, (block, 1), 0) < length
    d_out = jnp.where(live, cotangent_ref[0].astype(F32) + out - final_ref[0], 0.0)
    add(S_GAIN_TWO, column_sum(d_out * normed_two))
    add(S_SHIFT_TWO, column_sum(d_out))
    d_res_two = norm_back(d_out * vector(gain_two), normed_two, inverse_two)
    d_down = d_res_two.astype(BF16)
    d_down_ref[0] = d_down
    add(S_DOWN, column_sum(d_down.astype(F32)))
    d_up_in = jnp.zeros((block, D), F32)
    for c in range(CHUNKS):
        columns = slice(D * c, D * (c + 1))
        d_act = nt(d_down, w_down[columns, :])
        rise = slope[:, columns]
        above, below = rise > 2.0, rise < -2.0
        d_pre = jnp.where(jnp.logical_or(above, below), 0.0, rise * d_act).astype(BF16)
        d_pre_ref[0, :, columns] = d_pre
        add(S_CLIP_THREE, column_sum(jnp.where(above, d_act, jnp.where(below, -d_act, 0.0))))
        add(S_UP + c, column_sum(d_pre.astype(F32)))
        d_up_in = d_up_in + nt(d_pre, w_up[:, columns])
    above, below = h_one > clips[2], h_one < -clips[2]
    add(S_CLIP_TWO, column_sum(jnp.where(above, d_up_in, jnp.where(below, -d_up_in, 0.0))))
    d_h_one = d_res_two + jnp.where(jnp.abs(h_one) < clips[2], d_up_in, 0.0)
    add(S_GAIN_ONE, column_sum(d_h_one * normed_one))
    add(S_SHIFT_ONE, column_sum(d_h_one))
    d_res_one = norm_back(d_h_one * vector(gain_one), normed_one, inverse_one)
    d_res_ref[0] = d_res_one
    d_attn = d_res_one.astype(BF16)
    d_attn_ref[0] = d_attn
    add(S_OUT, column_sum(d_attn.astype(F32)))
    d_cut = nt(d_attn, w_out[...])
    context = context_ref[0]
    above, below = context > clips[1], context < -clips[1]
    add(S_CLIP_ONE, column_sum(jnp.where(above, d_cut, jnp.where(below, -d_cut, 0.0))))
    d_context = jnp.where(jnp.abs(context) < clips[1], d_cut, 0.0).astype(BF16)
    d_context_ref[0] = d_context
    product = d_context.astype(F32) * context
    high = product.astype(BF16)
    low = (product - high.astype(F32)).astype(BF16)
    shape = (S_ROWS, D)
    heads = lax.broadcasted_iota(jnp.int32, shape, 1) // HEAD_DIM == lax.broadcasted_iota(jnp.int32, shape, 0)
    ones = heads.astype(F32).astype(BF16)
    dots = nt(ones, high) + nt(ones, low)
    for pair in range(PAIRS):
        dots_ref[0, pair] = dots[2 * pair : 2 * pair + 2]


def weight_grads_kernel(act, d_down, up_in, d_pre, cut, d_attn, g_down, g_up, g_out):
    g_down[...] = tn(act[...], d_down[...]).astype(BF16)
    g_up[...] = tn(up_in[...], d_pre[...]).astype(BF16)

    @pl.when(pl.program_id(0) == 0)
    def _():
        g_out[...] = tn(cut[...], d_attn[...]).astype(BF16)


def student_back_kernel(
    lengths, clips, x_ref, qkv_ref, tqk_ref, log_ref, dots_ref, d_context_ref, d_res_ref, w_qkv,
    input_ref, g_qkv, sums_ref, a_in, d_joined,
):
    row = pl.program_id(0)
    tokens = x_ref.shape[1]
    length = lengths[row]
    here = pl.ds(pl.multiple_of(row * tokens, tokens), tokens)

    @pl.when(row == 0)
    def _():
        sums_ref[...] = jnp.zeros_like(sums_ref)

    @pl.loop(0, PAIRS)
    def _(pair):
        queries, keys, values = (qkv_ref[0, :, pair_columns(3 * pair + i)] for i in range(3))
        t_queries, t_keys = (tqk_ref[0, :, pair_columns(2 * pair + i)] for i in range(2))
        d_context = d_context_ref[0, :, pair_columns(pair)]
        grads = attend_pair_back(
            queries, keys, values, t_queries, t_keys, log_ref[0, pair], dots_ref[0, pair], d_context, length
        )
        for i in range(3):
            d_joined[here, pair_columns(3 * pair + i)] = grads[i]
        for i, at in ((0, Q_QUERY), (2, Q_VALUE)):
            sums_ref[at : at + 1, pair_columns(pair)] += column_sum(grads[i].astype(F32))

    bound = clips[0]
    x = x_ref[0].astype(F32)
    a_in[here, :] = jnp.clip(x, -bound, bound).astype(BF16)
    d_a = nt(d_joined[here, :], w_qkv[...])
    inside = jnp.where(jnp.abs(x) < bound, 1.0, jnp.where(jnp.abs(x) == bound, 0.5, 0.0))
    input_ref[0] = (d_res_ref[0] + d_a * inside).astype(BF16)
    outside = (1.0 - inside) * d_a
    sums_ref[Q_CLIP : Q_CLIP + 1] += column_sum(jnp.where(x > 0, outside, -outside))

    @pl.when(row == pl.num_programs(0) - 1)
    def _():
        for i in range(3):
            g_qkv[:, D * i : D * (i + 1)] = tn(a_in[...], d_joined[:, D * i : D * (i + 1)]).astype(BF16)


def rows_spec(tokens, width):
    return pl.BlockSpec((1, tokens, width), lambda r, *_: (r, 0, 0))


def whole_spec(shape):
    return pl.BlockSpec(shape, lambda *_: (0,) * len(shape), pipeline_mode=pl.Buffered(1))


def smem_spec():
    return pl.BlockSpec(memory_space=pltpu.SMEM)


def params(**more):
    return pltpu.CompilerParams(vmem_limit_bytes=VMEM_LIMIT, **more)


def shaped(shape, dtype):
    return jax.ShapeDtypeStruct(shape, dtype)


def teacher_pass(lengths, x, w_qkv, w_out, w_up, w_down):
    rows, tokens, _ = x.shape
    return pl.pallas_call(
        teacher_kernel,
        grid=(rows,),
        in_specs=[smem_spec(), rows_spec(tokens, D)] + [whole_spec(w.shape) for w in (w_qkv, w_out, w_up, w_down)],
        out_specs=[rows_spec(tokens, 2 * D), rows_spec(tokens, D)],
        out_shape=[shaped((rows, tokens, 2 * D), BF16), shaped((rows, tokens, D), F32)],
        scratch_shapes=[pltpu.VMEM((tokens, D), BF16)],
        compiler_params=params(),
    )(lengths, x, w_qkv, w_out, w_up, w_down)


def student_attend(lengths, clips, x, w_qkv, bias_q, bias_v):
    rows, tokens, _ = x.shape
    logs = (1, PAIRS, 2, tokens)
    return pl.pallas_call(
        student_attend_kernel,
        grid=(rows,),
        in_specs=[smem_spec(), smem_spec(), rows_spec(tokens, D), whole_spec(w_qkv.shape)] + [whole_spec((1, D))] * 2,
        out_specs=[
            rows_spec(tokens, 3 * D),
            rows_spec(tokens, D),
            pl.BlockSpec(logs, lambda r: (r, 0, 0, 0)),
        ],
        out_shape=[
            shaped((rows, tokens, 3 * D), BF16),
            shaped((rows, tokens, D), F32),
            shaped((rows,) + logs[1:], F32),
        ],
        scratch_shapes=[pltpu.VMEM((tokens, D), BF16)],
        compiler_params=params(),
    )(lengths, clips, x, w_qkv, bias_q.reshape(1, D), bias_v.reshape(1, D))


def student_middle(lengths, clips, x, cotangent, final, context, weights, vectors):
    rows, tokens, _ = x.shape
    block = tokens // 2 if tokens % 32 == 0 else tokens
    wide = {"act": FF, "d_pre": FF}
    names = ("mixed", "act", "d_pre", "up_in", "d_down", "cut", "d_attn", "d_res", "d_context")

    def spec(width):
        return pl.BlockSpec((1, block, width), lambda r, i: (r, i, 0))

    return pl.pallas_call(
        student_middle_kernel,
        grid=(rows, tokens // block),
        in_specs=[smem_spec(), smem_spec()]
        + [spec(D)] * 4
        + [whole_spec(w.shape) for w in (*weights, *vectors)],
        out_specs=[spec(wide.get(name, D)) for name in names]
        + [pl.BlockSpec((1, PAIRS, 2, block), lambda r, i: (r, 0, 0, i)), whole_spec((S_ROWS, D))],
        out_shape=[
            shaped((rows, tokens, wide.get(name, D)), F32 if name == "d_res" else BF16) for name in names
        ]
        + [shaped((rows, PAIRS, 2, tokens), F32), shaped((S_ROWS, D), F32)],
        scratch_shapes=[pltpu.VMEM((block, FF), F32)],
        compiler_params=params(),
    )(lengths, clips, x, cotangent, final, context, *weights, *vectors)


def weight_grads(act, d_down, up_in, d_pre, cut, d_attn):
    flat = [v.reshape(-1, v.shape[-1]) for v in (act, d_down, up_in, d_pre, cut, d_attn)]
    tokens = flat[0].shape[0]
    chunk = pl.BlockSpec((tokens, D), lambda c: (0, c))
    same = whole_spec((tokens, D))
    return pl.pallas_call(
        weight_grads_kernel,
        grid=(CHUNKS,),
        in_specs=[chunk, same, same, chunk, same, same],
        out_specs=[
            pl.BlockSpec((D, D), lambda c: (c, 0)),
            pl.BlockSpec((D, D), lambda c: (0, c)),
            whole_spec((D, D)),
        ],
        out_shape=[shaped((FF, D), BF16), shaped((D, FF), BF16), shaped((D, D), BF16)],
        compiler_params=params(),
    )(*flat)


def student_back(lengths, clips, x, qkv, tqk, logs, dots, d_context, d_res, w_qkv):
    rows, tokens, _ = x.shape
    return pl.pallas_call(
        student_back_kernel,
        grid=(rows,),
        in_specs=[smem_spec(), smem_spec(), rows_spec(tokens, D), rows_spec(tokens, 3 * D), rows_spec(tokens, 2 * D)]
        + [pl.BlockSpec((1,) + logs.shape[1:], lambda r: (r, 0, 0, 0))] * 2
        + [rows_spec(tokens, D), rows_spec(tokens, D), whole_spec(w_qkv.shape)],
        out_specs=[rows_spec(tokens, D), whole_spec((D, 3 * D)), whole_spec((Q_ROWS, D))],
        out_shape=[shaped((rows, tokens, D), BF16), shaped((D, 3 * D), BF16), shaped((Q_ROWS, D), F32)],
        scratch_shapes=[pltpu.VMEM((rows * tokens, D), BF16), pltpu.VMEM((rows * tokens, 3 * D), BF16)],
        compiler_params=params(),
    )(lengths, clips, x, qkv, tqk, logs, dots, d_context, d_res, w_qkv)


PLANES, COLUMNS, CORES = 4, 4, 2
DEVICES = PLANES * COLUMNS * CORES


class Place:
    def __init__(self):
        self.me = lax.axis_index("shard")
        self.core = self.me % 2
        self.x = (self.me // 2) % 2
        self.y = (self.me // 4) % 2
        self.z = self.me // 8
        self.column = (self.me // 2) % 4
        self.along_x = self.me + 2 - 4 * self.x
        self.along_y = self.me + 4 - 8 * self.y
        self.sibling = self.me + 1 - 2 * self.core
        self.along_a = self.along_x + (self.along_y - self.along_x) * self.core
        self.along_b = self.along_y + (self.along_x - self.along_y) * self.core

    def plane(self, step):
        return (self.me + 8 * step) % DEVICES

    def meet(self):
        partners = [self.sibling, self.along_x, self.along_y] + [self.plane(k) for k in range(1, PLANES)]
        barrier = pltpu.get_barrier_semaphore()
        for partner in partners:
            pl.semaphore_signal(barrier, inc=1, device_id=(partner,), device_id_type=MESH)
        pl.semaphore_wait(barrier, len(partners))


class Trip:
    SEMAPHORES = 14

    def __init__(self, place, source, out, rows, columns, early, send, receive):
        self.place, self.early, self.send, self.receive = place, early, send, receive
        self.source = source.at[rows, columns]
        height, size = source.shape[0], rows.stop - rows.start

        def where(column):
            start = pl.multiple_of(height * (column % CORES) + rows.start, 8)
            return column // CORES, pl.ds(start, size)

        def one(z, column):
            chip, inside = where(column)
            return out.at[z, chip, inside, columns]

        def slab_of(column):
            chip, inside = where(column)
            return out.at[:, chip, inside, columns]

        self.one, self.all = one, slab_of
        self.mine = place.me % 8
        self.at_a = self.mine + place.along_a - place.me
        self.at_b = self.mine + place.along_b - place.me
        self.at_ab = self.at_a + self.at_b - self.mine

    def remote(self, source, target, slot, device):
        return pltpu.make_async_remote_copy(
            src_ref=source, dst_ref=target, send_sem=self.send.at[slot], recv_sem=self.receive.at[slot],
            device_id=(device,), device_id_type=MESH,
        )

    def own(self):
        return pltpu.make_async_copy(self.source, self.one(self.place.z, self.mine), self.send.at[0])

    def line(self, step, source, column, slot):
        return self.remote(source, self.one(self.place.z, column), slot, self.place.plane(step))

    def line_from(self, step, column, slot):
        part = self.one((self.place.z + PLANES - step) % PLANES, column)
        return self.remote(part, part, slot, self.place.plane(step))

    def slab(self, column, slot, device):
        part = self.all(column)
        return self.remote(part, part, slot, device)

    def across(self, source, column):
        return self.remote(source, self.one(self.place.z, column), 4, self.place.along_a)

    def first(self):
        self.own().start()
        if self.early:
            self.across(self.source, self.mine).start()
        for step in range(1, PLANES):
            self.line(step, self.source, self.mine, step).start()

    def second(self):
        place = self.place
        self.own().wait()
        if self.early:
            part = self.one(place.z, self.at_a)
            self.across(part, self.at_a).wait_recv()
            for step in range(1, PLANES):
                self.line(step, part, self.at_a, 10 + step).start()
            return
        for step in range(1, PLANES):
            self.line_from(step, self.mine, step).wait_recv()
        self.slab(self.mine, 4, place.along_a).start()
        self.slab(self.mine, 5, place.along_b).start()
        self.slab(self.mine, 7, place.sibling).start()

    def third(self):
        place = self.place
        if self.early:
            for step in range(1, PLANES):
                self.line_from(step, self.mine, step).wait_recv()
                self.line_from(step, self.at_a, 10 + step).wait_recv()
            self.slab(self.mine, 5, place.along_b).start()
            self.slab(self.mine, 7, place.sibling).start()
        else:
            self.slab(self.at_a, 4, place.along_a).wait_recv()
        self.slab(self.at_a, 6, place.along_b).start()
        self.slab(self.at_a, 8, place.sibling).start()

    def fourth(self):
        place = self.place
        self.slab(self.at_b, 5, place.along_b).wait_recv()
        self.slab(self.at_b, 9, place.sibling).start()
        self.slab(self.at_ab, 6, place.along_b).wait_recv()
        self.slab(self.at_ab, 10, place.sibling).start()

    def fifth(self):
        for slot in range(7, 11):
            self.slab(self.mine, slot, self.place.sibling).wait_recv()

    def phases(self):
        return [self.first, self.second, self.third, self.fourth, self.fifth]

    def last(self):
        one = self.one(self.place.z, self.mine)
        for step in range(1, PLANES):
            self.line(step, one, self.mine, step).wait_send()
            if self.early:
                self.line(step, one, self.mine, 10 + step).wait_send()
        if self.early:
            self.across(one, self.mine).wait_send()
        for slot in range(5 if self.early else 4, 11):
            self.slab(self.mine, slot, self.place.sibling).wait_send()


T_QKV, T_OUT, T_UP, T_DOWN, B_QKV, B_OUT, B_UP, B_DOWN = range(8)
TRAVEL = ((T_QKV, 6), (B_QKV, 2), (T_DOWN, 2), (T_OUT, 1), (T_UP, 2), (B_OUT, 1), (B_DOWN, 1), (B_UP, 2))
EARLY = (T_OUT, B_OUT, B_UP,)
TALL = (T_DOWN, B_DOWN)
FORWARD_PLAN = (
    (0, 0, 0), (0, 1, 0), (0, 2, 0), (0, 3, 0), (0, 0, 1), (0, 4, 0), (0, 1, 1), (0, 5, 0), (0, 2, 1), (0, 6,
    0), (0, 0, 2), (0, 3, 1), (0, 1, 2), (0, 4, 1), (0, 2, 2), (0, 5, 1), (0, 0, 3), (0, 7, 0), (0, 3, 2), (0,
    6, 1), (0, 1, 3), (0, 0, 4), (0, 2, 3), (0, 4, 2), (0, 5, 2), (0, 8, 0), (0, 3, 3), (0, 1, 4), (1, 7, 1),
    (2, 2, 4), (2, 3, 4), (2, 6, 2), (3, 4, 3), (3, 5, 3), (3, 9, 0), (4, 8, 1), (5, 4, 4), (5, 5, 4), (5, 7,
    2), (6, 6, 3), (6, 10, 0), (8, 6, 4), (8, 9, 1), (8, 11, 0), (9, 10, 1), (10, 7, 3), (10, 8, 2), (13, 7, 4),
    (13, 12, 0), (14, 9, 2), (14, 10, 2), (14, 8, 3), (14, 11, 1), (16, 13, 0), (17, 8, 4), (18, 12, 1), (18,
    14, 0), (19, 13, 1), (19, 10, 3), (21, 10, 4), (23, 9, 3), (23, 11, 2), (24, 13, 2), (25, 12, 2), (25, 9,
    4), (25, 15, 0), (27, 11, 3), (27, 14, 1), (28, 13, 3), (28, 15, 1), (29, 11, 4), (30, 12, 3), (30, 13, 4),
    (31, 16, 0), (32, 12, 4), (33, 15, 2), (34, 16, 1), (36, 14, 2), (39, 15, 3), (39, 16, 2), (42, 14, 3), (42,
    15, 4), (44, 16, 3), (45, 14, 4), (46, 16, 4),
)


def travel_parts(shapes):
    parts = []
    for weight, pieces in TRAVEL:
        rows, width = shapes[weight]
        for i in range(pieces):
            if weight in TALL:
                parts.append((weight, slice(i * rows // pieces, (i + 1) * rows // pieces), slice(0, width)))
            else:
                lanes = width // 128
                columns = slice(i * lanes // pieces * 128, (i + 1) * lanes // pieces * 128)
                parts.append((weight, slice(0, rows), columns))
    return parts


def forward_kernel(*refs):
    lengths, clips = refs[:2]
    teacher_hbm, hidden_hbm = refs[2:4]
    teach, latent, (bias_q, bias_v) = refs[4:8], refs[8:12], refs[12:14]
    outs = refs[14:22]
    tqk_hbm, final_hbm, qkv_hbm, context_hbm, log_hbm = refs[22:27]
    low, near, biases = refs[27:32], refs[32:37], refs[37]
    t_x, a_in, tqk, t_context, final, qkv, context, logs = refs[38:46]
    send, receive, load, store = refs[46:]
    rows = t_x.shape[0]
    place = Place()
    inputs = [pltpu.make_async_copy(teacher_hbm, t_x, load.at[0]), pltpu.make_async_copy(hidden_hbm, a_in, load.at[1])]
    for copy in inputs:
        copy.start()
    for pair in range(PAIRS):
        for i in range(3):
            to, at = TRIPLE * pair + PAIR * i, D * i + PAIR * pair
            low[4][:, to : to + PAIR] = teach[0][:, at : at + PAIR]
    place.meet()
    sources = [low[4], *teach[1:], *low[:4]]
    parts = travel_parts([source.shape for source in sources])
    trips = [
        Trip(place, sources[w], outs[w], r, c, w in EARLY, send.at[i], receive.at[i])
        for i, (w, r, c) in enumerate(parts)
    ]
    weights = [w for w, _, _ in parts]

    def landing(i):
        weight, r, c = parts[i]
        if weight in TALL:
            c = slice(0, near[weight].shape[1])
        flat = outs[weight].reshape(near[weight].shape)
        return pltpu.make_async_copy(flat.at[:, c], near[weight].at[:, c], load.at[2 + i])

    def lands(i):
        weight = weights[i]
        return weight <= B_QKV and (weight not in TALL or weight not in weights[i + 1 :])

    def binarize():
        for i in range(1, 4):
            low[i][...] = signed_mean(latent[i][...])
        b_qkv = signed_mean(latent[0][...])
        for pair in range(PAIRS):
            for i in range(3):
                to, at = TRIPLE * pair + PAIR * i, D * i + PAIR * pair
                low[0][:, to : to + PAIR] = b_qkv[:, at : at + PAIR]
        biases[0:1] = bias_q[...].reshape(1, D)
        biases[1:2] = bias_v[...].reshape(1, D)

    phases = [trip.phases() for trip in trips]
    first_student = next(at for at, (_, i, _) in enumerate(FORWARD_PLAN) if weights[i] >= B_QKV)

    def do(at):
        _, i, phase = FORWARD_PLAN[at]
        if at == first_student:
            binarize()
        phases[i][phase]()
        if phase == 4 and lands(i):
            landing(i).start()

    counts = (PAIRS * rows, PAIRS * rows, CHUNKS * rows)
    stage_two, stage_three, end = counts[0], counts[0] + counts[1], sum(counts)
    per = {weight: [i for i, w in enumerate(weights) if w == weight and lands(i)] for weight in set(weights)}

    def stage(slot):
        for at, (when, _, _) in enumerate(FORWARD_PLAN):
            if when == slot:
                do(at)

    def turn(first_slot, count, index):
        for slot in sorted({when for when, _, _ in FORWARD_PLAN if first_slot <= when < first_slot + count}):
            pl.when(index == slot - first_slot)(functools.partial(stage, slot))

    def await_parts(weight, pair, row):
        pairs_each = PAIRS // len(per[weight])
        for n, part in enumerate(per[weight]):
            pl.when(jnp.logical_and(pair == n * pairs_each, row == 0))(landing(part).wait)

    def out_copy(source, target, slot, row):
        return pltpu.make_async_copy(source.at[row], target.at[row], store.at[slot, row])

    inputs[0].wait()
    inputs[1].wait()

    @pl.loop(0, rows)
    def _(row):
        a_in[row] = jnp.clip(a_in[row].astype(F32), -clips[0], clips[0]).astype(BF16)

    @pl.loop(0, PAIRS)
    def _(pair):
        @pl.loop(0, rows)
        def _(row):
            turn(0, counts[0], pair * rows + row)
            await_parts(T_QKV, pair, row)
            teacher_pair(pair, t_x[row], lengths[row], near[T_QKV], tqk.at[row], t_context.at[row])

    for row in range(rows):
        out_copy(tqk, tqk_hbm, 0, row).start()

    @pl.loop(0, PAIRS)
    def _(pair):
        @pl.loop(0, rows)
        def _(row):
            turn(stage_two, counts[1], pair * rows + row)
            await_parts(B_QKV, pair, row)
            student_pair(
                pair, a_in[row], lengths[row], near[B_QKV], biases.at[0:1], biases.at[1:2],
                qkv.at[row], context.at[row], logs.at[row],
            )

    for row in range(rows):
        out_copy(qkv, qkv_hbm, 2, row).start()
        out_copy(context, context_hbm, 3, row).start()
        out_copy(logs, log_hbm, 4, row).start()
    stage(stage_three)
    for weight in (T_OUT, T_UP, T_DOWN):
        for part in per[weight]:
            landing(part).wait()

    @pl.loop(0, rows)
    def _(row):
        final[row] = teacher_last(
            t_x[row], t_context[row], near[T_OUT], near[T_UP], near[T_DOWN],
            lambda c: turn(stage_three + 1, counts[2] - 1, row * CHUNKS + c - 1),
        )
        out_copy(final, final_hbm, 1, row).start()

    stage(end)
    for trip in trips:
        trip.last()

    @pl.loop(0, rows)
    def _(row):
        for slot, (source, target) in enumerate(
            ((tqk, tqk_hbm), (final, final_hbm), (qkv, qkv_hbm), (context, context_hbm), (logs, log_hbm))
        ):
            out_copy(source, target, slot, row).wait()


def forward_pass(lengths, clips, teacher_input, hidden, teach, latent, bias_q, bias_v):
    rows, tokens, _ = hidden.shape
    anywhere, vmem = pl.BlockSpec(memory_space=pl.ANY), pl.BlockSpec(memory_space=pltpu.VMEM)
    gathered = [(PLANES, COLUMNS, CORES * w.shape[0], w.shape[1]) for w in teach] * 2
    made = [
        shaped((rows, tokens, 2 * D), BF16),
        shaped((rows, tokens, D), F32),
        shaped((rows, tokens, 3 * D), BF16),
        shaped((rows, tokens, D), F32),
        shaped((rows, PAIRS, 2, tokens), F32),
    ]
    parts = sum(pieces for _, pieces in TRAVEL)
    near = [(DEVICES * w.shape[0], w.shape[1]) for w in teach] + [(DEVICES * teach[0].shape[0], 3 * D)]
    x_scratch = pltpu.VMEM((rows, tokens, D), BF16)
    outs = pl.pallas_call(
        forward_kernel,
        in_specs=[smem_spec(), smem_spec()] + [anywhere] * 2 + [vmem] * 10,
        out_specs=[anywhere] * 13,
        out_shape=[shaped(shape, BF16) for shape in gathered] + made,
        scratch_shapes=[pltpu.VMEM(w.shape, BF16) for w in (*latent, teach[0])]
        + [pltpu.VMEM(shape, BF16) for shape in near]
        + [pltpu.VMEM((8, D), F32), x_scratch, x_scratch]
        + [pltpu.VMEM(made[0].shape, BF16), x_scratch]
        + [pltpu.VMEM(m.shape, m.dtype) for m in made[1:]]
        + [pltpu.SemaphoreType.DMA((parts, Trip.SEMAPHORES))] * 2
        + [pltpu.SemaphoreType.DMA((2 + parts,)), pltpu.SemaphoreType.DMA((5, rows))],
        compiler_params=params(collective_id=0, has_side_effects=True),
    )(lengths, clips, teacher_input, hidden, *teach, *latent, bias_q, bias_v)
    weights = [out.reshape(-1, out.shape[-1]) for out in outs[4:8]]
    return weights, outs[8:]


class Fold:
    SEMAPHORES = 8

    def __init__(self, place, grad, own, finish, buffers, send, receive):
        self.place, self.grad, self.own, self.finish = place, grad, own, finish
        self.from_core, self.to_p, self.from_p, self.to_q, self.from_q, self.to_z, self.from_z = buffers
        self.send, self.receive = send, receive
        core = place.core
        self.p_stride, self.q_stride = 1 + core, 2 - core
        self.p = place.x + (place.y - place.x) * core
        self.q = place.y + (place.x - place.y) * core

    def remote(self, source, target, slot, device):
        return pltpu.make_async_remote_copy(
            src_ref=source, dst_ref=target, send_sem=self.send.at[slot], recv_sem=self.receive.at[slot],
            device_id=(device,), device_id_type=MESH,
        )

    def column(self, p, q):
        return p * self.p_stride + q * self.q_stride

    def keep(self):
        return pltpu.make_async_copy(self.grad.at[:, :, self.place.core], self.own, self.send.at[0])

    def over_core(self):
        return self.remote(self.grad.at[:, :, 1 - self.place.core], self.from_core, 1, self.place.sibling)

    def over_p(self):
        return self.remote(self.to_p, self.from_p, 2, self.place.along_a)

    def over_q(self):
        return self.remote(self.to_q, self.from_q, 3, self.place.along_b)

    def over_z(self, step):
        return self.remote(self.to_z.at[step - 1], self.from_z.at[step - 1], 3 + step, self.place.plane(step))

    def mine(self, z, column):
        return self.grad[z, column, self.place.core] if self.own is None else self.own[z, column]

    def pair_sum(self, z, column):
        return self.mine(z, column).astype(F32) + self.from_core[z, column].astype(F32)

    def first(self):
        if self.own is not None:
            self.keep().start()
        self.over_core().start()

    def second(self):
        if self.own is not None:
            self.keep().wait()
        self.over_core().wait_recv()

        @pl.loop(0, 2 * PLANES)
        def _(i):
            z, q = i // 2, i % 2
            column = self.column(1 - self.p, q)
            self.to_p[z, q] = self.mine(z, column) + self.from_core[z, column]

        self.over_p().start()

    def third(self):
        self.over_p().wait_recv()

        @pl.loop(0, PLANES)
        def _(z):
            q = 1 - self.q
            total = self.pair_sum(z, self.column(self.p, q)) + self.from_p[z, q].astype(F32)
            self.to_q[z] = total.astype(BF16)

        self.over_q().start()

    def quad_sum(self, z):
        q = self.q
        total = self.pair_sum(z, self.column(self.p, q)) + self.from_p[z, q].astype(F32)
        return total + self.from_q[z].astype(F32)

    def fourth(self):
        self.over_q().wait_recv()
        for step in range(1, PLANES):
            self.to_z[step - 1] = self.quad_sum((self.place.z + step) % PLANES).astype(BF16)
            self.over_z(step).start()

    def fifth(self):
        total = self.quad_sum(self.place.z)
        for step in range(1, PLANES):
            self.over_z(step).wait_recv()
            total = total + self.from_z[step - 1].astype(F32)
        self.finish(total)

    def phases(self):
        return [self.first, self.second, self.third, self.fourth, self.fifth]

    def last(self):
        self.over_core().wait_send()
        self.over_p().wait_send()
        self.over_q().wait_send()
        for step in range(1, PLANES):
            self.over_z(step).wait_send()


FOLD_BUFFERS = ((4, 4), (4, 2), (4, 2), (4,), (4,), (3,), (3,))


class Share:
    SEMAPHORES = 7

    def __init__(self, place, value, out, partial, received, send, receive):
        self.place, self.value, self.out = place, value, out
        self.partial, self.received, self.send, self.receive = partial, received, send, receive

    def swap(self, slot, device):
        return pltpu.make_async_remote_copy(
            src_ref=self.partial.at[min(slot, 3)], dst_ref=self.received.at[slot], send_sem=self.send.at[slot],
            recv_sem=self.receive.at[slot], device_id=(device,), device_id_type=MESH,
        )

    def partners(self):
        place = self.place
        return [place.sibling, place.along_x, place.along_y] + [place.plane(k) for k in range(1, PLANES)]

    def first(self):
        self.partial[0] = self.value[...]
        self.swap(0, self.place.sibling).start()

    def step(self, at):
        partners = self.partners()
        self.swap(at, partners[at]).wait_recv()
        self.partial[at + 1] = self.partial[at] + self.received[at]
        for slot in (at + 1,) if at < 2 else (3, 4, 5):
            self.swap(slot, partners[slot]).start()

    def finish(self):
        partners = self.partners()
        for slot in (3, 4, 5):
            self.swap(slot, partners[slot]).wait_recv()
        place = self.place
        self.received[6] = self.partial[3]
        total = jnp.zeros(self.value.shape, F32)
        for z in range(PLANES):
            behind = (place.z + PLANES - z) % PLANES
            total = total + self.received[(behind + 3) % PLANES + 3]
        self.out[...] = total

    def phases(self):
        return [self.first] + [functools.partial(self.step, at) for at in range(3)] + [self.finish]

    def last(self):
        for slot, partner in enumerate(self.partners()):
            self.swap(slot, partner).wait_send()


GRAD_STEPS = 2 * CHUNKS + 1
FOLDED = ((0, 4), (1, 4), (2, 1))
FOLD_PARTS = sum(pieces for _, pieces in FOLDED)
BACKWARD_PLAN = (
    (5, 0, 0), (5, 1, 0), (5, 2, 0), (5, 3, 0), (6, 4, 0), (7, 5, 0), (8, 6, 0), (9, 0, 1), (9, 7, 0), (9, 8,
    0), (11, 1, 1), (12, 9, 0), (12, 0, 2), (12, 2, 1), (12, 15, 0), (14, 1, 2), (14, 3, 1), (14, 9, 1), (14,
    15, 1), (15, 10, 0), (15, 0, 3), (15, 2, 2), (16, 15, 2), (17, 1, 3), (17, 4, 1), (17, 10, 1), (17, 9, 2),
    (18, 11, 0), (18, 0, 4), (18, 2, 3), (18, 3, 2), (18, 15, 3), (19, 5, 1), (19, 1, 4), (19, 9, 3), (20, 10,
    2), (20, 11, 1), (21, 12, 0), (21, 3, 3), (21, 4, 2), (21, 6, 1), (21, 15, 4), (22, 2, 4), (22, 5, 2), (22,
    9, 4), (22, 10, 3), (22, 11, 2), (23, 12, 1), (24, 13, 0), (24, 3, 4), (24, 4, 3), (24, 7, 1), (24, 10, 4),
    (24, 11, 3), (25, 5, 3), (25, 6, 2), (25, 12, 2), (26, 8, 1), (26, 13, 1), (27, 14, 0), (27, 7, 2), (27, 6,
    3), (27, 11, 4), (27, 12, 3), (28, 4, 4), (29, 5, 4), (30, 8, 2), (30, 13, 2), (30, 14, 1), (30, 16, 0),
    (30, 7, 3), (30, 12, 4), (30, 16, 1), (30, 6, 4), (30, 13, 3), (30, 7, 4), (30, 16, 2), (30, 8, 3), (30, 14,
    2), (30, 13, 4), (30, 16, 3), (30, 14, 3), (30, 8, 4), (30, 16, 4), (30, 14, 4),
)


def fold_parts(shapes):
    parts = []
    for i, pieces in FOLDED:
        rows, width = shapes[i]
        for at in range(pieces):
            if i == 0:
                size = rows // pieces
                parts.append((i, slice(at * size, (at + 1) * size), slice(0, width), (size, width)))
            else:
                size = width // pieces
                parts.append((i, slice(0, rows), slice(at * size, (at + 1) * size), (rows, size)))
    return parts


def backward_kernel(*refs):
    lengths, clips = refs[:2]
    qkv, tqk, logs, dots, d_context, w_triple = refs[2:8]
    (x_hbm, d_res_hbm), (act, d_down, up_in, d_pre, cut, d_attn), sums = refs[8:10], refs[10:16], refs[16]
    input_hbm, grads = refs[17], refs[18:21]
    g_down, g_up, g_out, g_qkv, sums_out, q_sums_out = refs[21:27]
    x, a_in_t, d_pair, d_a, d_res, g_pair, q_sums, ring, stage_tall, stage_wide = refs[27:37]
    scratch = refs[37:]
    rows, tokens = qkv.shape[0], qkv.shape[1]
    place = Place()
    at_step = pl.program_id(0)
    at_pair = at_step - GRAD_STEPS
    parts = fold_parts([g_down.shape, g_up.shape, g_out.shape])
    owns, scratch = scratch[:FOLD_PARTS], scratch[FOLD_PARTS:]
    per = len(FOLD_BUFFERS)
    taken = (FOLD_PARTS + PAIRS) * per
    buffers, (s_partial, s_received, q_partial, q_received, send, receive, load) = scratch[:taken], scratch[taken:]

    def set_part(target, r, c):
        def finish(total):
            target[r, c] = total

        return finish

    def set_triple(pair):
        def finish(total):
            for i in range(3):
                at = D * i + PAIR * pair
                g_qkv[:, at : at + PAIR] = total[:, PAIR * i : PAIR * (i + 1)]

        return finish

    folds = []
    for n, (i, r, c, _) in enumerate(parts):
        target = (g_down, g_up, g_out)[i]
        source = grads[i].at[:, :, :, r, c]
        folds.append(
            Fold(place, source, owns[n], set_part(target, r, c), buffers[per * n : per * n + per], send.at[n], receive.at[n])
        )
    for pair in range(PAIRS):
        n = FOLD_PARTS + pair
        folds.append(
            Fold(
                place, g_pair.at[pair], None, set_triple(pair), buffers[per * n : per * n + per], send.at[n], receive.at[n]
            )
        )
    n = len(folds)
    share = Share(place, sums, sums_out, s_partial, s_received, send.at[n], receive.at[n])
    q_share = Share(place, q_sums, q_sums_out, q_partial, q_received, send.at[n + 1], receive.at[n + 1])
    inputs = [pltpu.make_async_copy(x_hbm, x, load.at[0]), pltpu.make_async_copy(d_res_hbm, d_res, load.at[1])]

    slots = GRAD_STEPS + PAIRS * rows
    phases = [fold.phases() for fold in folds] + [share.phases(), q_share.phases()]
    timed = [
        (slot, phases[i][phase]) for slot, i, phase in BACKWARD_PLAN if phase or not FOLD_PARTS <= i < FOLD_PARTS + PAIRS
    ]

    def stage(slot):
        for when, act in timed:
            if when == slot:
                act()

    def turn(index):
        for slot in sorted({when for when, _ in timed if when < slots}):
            pl.when(index == slot)(functools.partial(stage, slot))

    def load_left(source):
        return pltpu.make_async_copy(source, x, load.at[2])

    def chunk(source, c, step):
        part = source.at[:, :, pl.ds(pl.multiple_of(c * D, D), D)]
        return pltpu.make_async_copy(part, ring.at[step % 2], load.at[3 + step % 2])

    def load_chunk(step):
        pl.when(step < CHUNKS)(lambda: chunk(act, step, step).start())
        pl.when(jnp.logical_and(step >= CHUNKS, step < 2 * CHUNKS))(lambda: chunk(d_pre, step - CHUNKS, step).start())
        pl.when(step == 2 * CHUNKS)(lambda: chunk(d_attn, 0, step).start())

    def tall_out(c):
        return pltpu.make_async_copy(stage_tall, grads[0].at[c], load.at[5])

    def wide_out(c):
        columns = pl.ds(pl.multiple_of(c * D, D), D)
        return pltpu.make_async_copy(stage_wide, grads[1].at[:, :, :, :, columns], load.at[6])

    out_out = pltpu.make_async_copy(stage_wide, grads[2], load.at[6])

    @pl.when(at_step == 0)
    def _():
        load_left(d_down).start()
        load_chunk(0)
        inputs[1].start()
        place.meet()
        q_sums[...] = jnp.zeros_like(q_sums)
        d_a[...] = jnp.zeros_like(d_a)

    @pl.when(at_step < GRAD_STEPS)
    def _():
        turn(at_step)
        for step, following in ((0, up_in), (CHUNKS, cut), (2 * CHUNKS, None)):

            @pl.when(at_step == step)
            def _():
                load_left(d_down).wait()
                a_in_t[...] = x[...].reshape(rows * tokens, D).T
                (inputs[0] if following is None else load_left(following)).start()

        chunk(act, 0, at_step).wait()
        load_chunk(at_step + 1)
        product = nn(a_in_t[...], ring[at_step % 2].reshape(rows * tokens, D))

        @pl.when(at_step < CHUNKS)
        def _():
            pl.when(at_step > 0)(tall_out(0).wait)
            stage_tall[...] = product.T.reshape(stage_tall.shape).astype(BF16)
            tall_out(at_step).start()

        @pl.when(at_step >= CHUNKS)
        def _():
            pl.when(at_step == CHUNKS)(tall_out(0).wait)
            pl.when(at_step > CHUNKS)(wide_out(0).wait)
            height = stage_wide.shape[3]
            for device in range(DEVICES):
                z, column, core = device // 8, device // 2 % COLUMNS, device % CORES
                stage_wide[z, column, core] = product[height * device : height * (device + 1)].astype(BF16)
            pl.when(at_step < 2 * CHUNKS)(lambda: wide_out(at_step - CHUNKS).start())
            pl.when(at_step == 2 * CHUNKS)(out_out.start)

    pl.when(at_step == GRAD_STEPS)(out_out.wait)

    def pair_step():
        one_pair(
            lengths, clips, at_pair, turn, stage, slots, folds, timed, share, q_share, inputs, input_hbm, load,
            qkv, tqk, logs, dots, d_context, w_triple, g_qkv.shape[0], x, a_in_t, d_pair, d_a, d_res, g_pair, q_sums,
        )

    pl.when(at_pair >= 0)(pair_step)


def one_pair(
    lengths, clips, at_pair, turn, stage, slots, folds, timed, share, q_share, inputs, input_hbm, load,
    qkv, tqk, logs, dots, d_context, w_triple, height, x, a_in_t, d_pair, d_a, d_res, g_pair, q_sums,
):
    rows, tokens = qkv.shape[0], qkv.shape[1]

    @pl.loop(0, rows)
    def _(row):
        turn(GRAD_STEPS + at_pair * rows + row)
        queries, keys, values = (qkv[row, :, PAIR * i : PAIR * (i + 1)] for i in range(3))
        t_queries, t_keys = (tqk[row, :, PAIR * i : PAIR * (i + 1)] for i in range(2))
        grads_here = attend_pair_back(
            queries, keys, values, t_queries, t_keys, logs[row, 0], dots[row, 0], d_context[row], lengths[row]
        )
        here = pl.ds(pl.multiple_of(row * tokens, tokens), tokens)
        for i in range(3):
            d_pair[here, PAIR * i : PAIR * (i + 1)] = grads_here[i]

    bound = clips[0]

    @pl.when(at_pair == 0)
    def _():
        inputs[0].wait()
        for row in range(rows):
            clipped = jnp.clip(x[row].astype(F32), -bound, bound)
            a_in_t[:, tokens * row : tokens * (row + 1)] = clipped.T.astype(BF16)

    g_now = nn(a_in_t[...], d_pair[...])
    for device in range(DEVICES):
        z, column, core = device // 8, device // 2 % COLUMNS, device % CORES
        g_pair[at_pair, z, column, core] = g_now[height * device : height * (device + 1)].astype(BF16)
    for pair, fold in enumerate(folds[FOLD_PARTS:]):
        pl.when(at_pair == pair)(fold.first)
    here = pair_columns(at_pair)
    q_sums[Q_QUERY : Q_QUERY + 1, here] = column_sum(d_pair[:, :PAIR].astype(F32))
    q_sums[Q_VALUE : Q_VALUE + 1, here] = column_sum(d_pair[:, 2 * PAIR :].astype(F32))
    d_a[...] += nt(d_pair[...], w_triple[...])

    @pl.when(at_pair == PAIRS - 1)
    def _():
        inputs[1].wait()
        for row in range(rows):
            stage(slots + row)
            value = x[row].astype(F32)
            d_row = d_a[tokens * row : tokens * (row + 1)]
            inside = jnp.where(jnp.abs(value) < bound, 1.0, jnp.where(jnp.abs(value) == bound, 0.5, 0.0))
            outside = (1.0 - inside) * d_row
            q_sums[Q_CLIP : Q_CLIP + 1] += column_sum(jnp.where(value > 0, outside, -outside))
            x[row] = (d_res[row] + d_row * inside).astype(BF16)
        out = pltpu.make_async_copy(x, input_hbm, load.at[0])
        out.start()
        for when, act in timed:
            if when >= slots + rows:
                act()
        for fold in folds:
            fold.last()
        share.last()
        q_share.last()
        out.wait()


def backward_pass(lengths, clips, hidden, qkv, tqk, logs, dots, d_context, d_res, w_qkv, made_by, sums):
    rows, tokens, _ = hidden.shape
    shapes = [(FF // DEVICES, D), (D // DEVICES, FF), (D // DEVICES, D)]
    height = w_qkv.shape[0] // DEVICES
    part_shapes = [part[3] for part in fold_parts(shapes)]
    fold_shapes = part_shapes + [(height, TRIPLE)] * PAIRS
    anywhere = pl.BlockSpec(memory_space=pl.ANY)

    def of_pair(width):
        return pl.BlockSpec((rows, tokens, width), lambda s: (0, 0, pair_at(s)))

    def pair_at(step):
        return step // GRAD_STEPS * (step - GRAD_STEPS)

    stat = pl.BlockSpec((rows, 1, 2, tokens), lambda s: (0, pair_at(s), 0, 0))
    small = [shaped(sums.shape, F32), shaped((Q_ROWS, D), F32)]
    made = [shaped(s, F32) for s in shapes] + [shaped((height, 3 * D), F32)] + small
    return pl.pallas_call(
        backward_kernel,
        grid=(GRAD_STEPS + PAIRS,),
        in_specs=[smem_spec(), smem_spec()]
        + [of_pair(TRIPLE), of_pair(DOUBLE), stat, stat, of_pair(PAIR), pl.BlockSpec((D, TRIPLE), lambda s: (0, pair_at(s)))]
        + [anywhere] * 8
        + [whole_spec(sums.shape)],
        out_specs=[anywhere] * 4 + [whole_spec(m.shape) for m in made],
        out_shape=[shaped(hidden.shape, BF16)]
        + [shaped((PLANES, COLUMNS, CORES) + shape, BF16) for shape in shapes]
        + made,
        scratch_shapes=[
            pltpu.VMEM((rows, tokens, D), BF16),
            pltpu.VMEM((D, rows * tokens), BF16),
            pltpu.VMEM((rows * tokens, TRIPLE), BF16),
            pltpu.VMEM((rows * tokens, D), F32),
            pltpu.VMEM((rows, tokens, D), F32),
            pltpu.VMEM((PAIRS, PLANES, COLUMNS, CORES, height, TRIPLE), BF16),
            pltpu.VMEM((Q_ROWS, D), F32),
            pltpu.VMEM((2, rows, tokens, D), BF16),
            pltpu.VMEM((COLUMNS, CORES) + shapes[0], BF16),
            pltpu.VMEM((PLANES, COLUMNS, CORES) + shapes[2], BF16),
        ]
        + [pltpu.VMEM((PLANES, COLUMNS) + s, BF16) for s in part_shapes]
        + [pltpu.VMEM(lead + s, BF16) for s in fold_shapes for lead in FOLD_BUFFERS]
        + [pltpu.VMEM((n,) + m.shape, F32) for m in small for n in (4, 7)]
        + [pltpu.SemaphoreType.DMA((len(fold_shapes) + 2, Fold.SEMAPHORES))] * 2
        + [pltpu.SemaphoreType.DMA((7,))],
        compiler_params=params(collective_id=1, has_side_effects=True),
    )(
        lengths, clips, qkv, tqk, logs, dots, d_context, w_qkv, hidden, d_res, *made_by, sums
    )


def finish_kernel(sums, q_sums, *refs):
    grads, input_hbm = refs[:4], refs[4]
    outs, input_out = refs[5:9], refs[9]
    b_q, b_v, b_out, b_up, b_down, gain_one, shift_one, gain_two, shift_two, clips = refs[10:20]
    held, arrive = refs[20:]
    copy = pltpu.make_async_copy(input_hbm, held, arrive)
    copy.start()

    def row(ref, at):
        return ref[at : at + 1].reshape(D)

    for source, target in zip(grads, outs):
        target[...] = source[...]
    b_q[...] = row(q_sums, Q_QUERY)
    b_v[...] = row(q_sums, Q_VALUE)
    b_out[...] = row(sums, S_OUT)
    b_up[...] = jnp.concatenate([sums[S_UP + c : S_UP + c + 1] for c in range(CHUNKS)], axis=1).reshape(FF)
    b_down[...] = row(sums, S_DOWN)
    gain_one[...] = row(sums, S_GAIN_ONE)
    shift_one[...] = row(sums, S_SHIFT_ONE)
    gain_two[...] = row(sums, S_GAIN_TWO)
    shift_two[...] = row(sums, S_SHIFT_TWO)
    clips[0] = jnp.sum(q_sums[Q_CLIP : Q_CLIP + 1])
    for i, at in enumerate((S_CLIP_ONE, S_CLIP_TWO, S_CLIP_THREE)):
        clips[1 + i] = jnp.sum(sums[at : at + 1])
    copy.wait()
    back = pltpu.make_async_copy(held, input_out, arrive)
    back.start()
    back.wait()


def finish(sums, q_sums, grads, input_grad):
    vmem, anywhere = pl.BlockSpec(memory_space=pltpu.VMEM), pl.BlockSpec(memory_space=pl.ANY)
    lengths = [D, D, D, FF, D, D, D, D, D]
    return pl.pallas_call(
        finish_kernel,
        in_specs=[vmem] * 6 + [anywhere],
        out_specs=[vmem] * 4 + [anywhere] + [vmem] * 9 + [smem_spec()],
        out_shape=[shaped(g.shape, F32) for g in grads]
        + [shaped(input_grad.shape, BF16)]
        + [shaped((n,), F32) for n in lengths]
        + [shaped((4,), F32)],
        scratch_shapes=[pltpu.VMEM(input_grad.shape, BF16), pltpu.SemaphoreType.DMA],
        compiler_params=params(),
    )(sums, q_sums, *grads, input_grad)


def on_device(
    by_kernel,
    hidden, teacher_input, cotangent, lengths, lat_qkv, lat_out, lat_up, lat_down,
    bias_q, bias_v, bias_out, bias_up, bias_down, gain_one, shift_one, gain_two, shift_two, clips,
    teach_qkv, teach_out, teach_up, teach_down,
):
    latent = (lat_qkv, lat_out, lat_up, lat_down)
    teach = (teach_qkv, teach_out, teach_up, teach_down)
    if by_kernel:
        (w_qkv, *weights), (tqk, final, qkv, context, logs) = forward_pass(
            lengths, clips, teacher_input, hidden, teach, latent, bias_q, bias_v
        )
    else:
        gather = functools.partial(lax.all_gather, axis_name="shard", axis=0, tiled=True)
        w_qkv, *weights = (gather(signed_mean(w)) for w in latent)
        w_qkv = by_pairs(w_qkv)
        t_qkv, *t_weights = (gather(w) for w in teach)
        tqk, final = teacher_pass(lengths, teacher_input, by_pairs(t_qkv), *t_weights)
        qkv, context, logs = student_attend(lengths, clips, hidden, w_qkv, bias_q, bias_v)
    vectors = (bias_out, bias_up, bias_down, gain_one, shift_one, gain_two, shift_two)
    mixed, act, d_pre, up_in, d_down, cut, d_attn, d_res, d_context, dots, sums = student_middle(
        lengths, clips, hidden, cotangent, final, context, weights, vectors
    )
    made_by = (act, d_down, up_in, d_pre, cut, d_attn)
    if by_kernel:
        input_grad, _, _, _, g_down, g_up, g_out, g_qkv, sums, q_sums = backward_pass(
            lengths, clips, hidden, qkv, tqk, logs, dots, d_context, d_res, w_qkv, made_by, sums
        )
    else:
        g_down, g_up, g_out = weight_grads(*made_by)
        input_grad, g_qkv, q_sums = student_back(lengths, clips, hidden, qkv, tqk, logs, dots, d_context, d_res, w_qkv)
        scatter = functools.partial(lax.psum_scatter, axis_name="shard", scatter_dimension=0, tiled=True)
        g_down, g_up, g_qkv, g_out = (scatter(g.astype(F32)) for g in (g_down, g_up, by_kinds(g_qkv), g_out))
        sums, q_sums = lax.psum((sums, q_sums), "shard")
    g_qkv, g_out, g_up, g_down, input_grad, *small = finish(sums, q_sums, (g_qkv, g_out, g_up, g_down), input_grad)
    return mixed, input_grad, g_qkv, g_out, g_up, g_down, *small


def solution(mesh):
    split, rows, same = P("shard", None), P("shard", None, None), P()
    return jax.shard_map(
        functools.partial(on_device, mesh.shape["shard"] == DEVICES),
        mesh=mesh,
        in_specs=(rows, rows, rows, P("shard")) + (split,) * 4 + (same,) * 10 + (split,) * 4,
        out_specs=(rows, rows) + (split,) * 4 + (same,) * 10,
        check_vma=False,
    )
```

profile of v0, /device:TPU:0, one launch (start us, length us, event | category | flops | bytes accessed | tf_op | source)
XLA Modules:
  0.0 340.4 jit_solution(17960936577912481662)
XLA Ops:
  0.7 140.0 %shard_map.333 = (bf16[4,4,48,2304]{3,2,1,0:T(8,128)(2,1)}, bf16[4,4,48,768]{3,2,1,0:T(8,128)(2,1)}, bf16[4,4,48,3072]{3,2,1,0:T(8,128)(2,1)}, bf16[4,4,192,768]...) custom-call(s32[3]{0:T(128)} %refs_0_.3, ...), custom_call_target="tpu_custom_call" | custom-call | tf_op jit(solution)/shard_map/pallas_call | solution.py:771
  140.6 65.8 %shard_map.334 = (bf16[3,512,768]{2,1,0:T(8,128)(2,1)}, bf16[3,512,3072]{2,1,0:T(8,128)(2,1)}, bf16[3,512,3072]{2,1,0:T(8,128)(2,1)}, bf16[3,512,768]{2,1,0:T(8,...) custom-call(s32[3]{0:T(128)} %refs_0_.3, ...), custom_call_target="tpu_custom_call" | custom-call | tf_op jit(solution)/shard_map/pallas_call | solution.py:396
  206.4 128.4 %shard_map.335 = (bf16[3,512,768]{2,1,0:T(8,128)(2,1)}, bf16[4,4,2,96,768]{4,3,2,1,0:T(8,128)(2,1)}, bf16[4,4,2,24,3072]{4,3,2,1,0:T(8,128)(2,1)}, bf16[4,4,2,24...) custom-call(s32[3]{0:T(128)} %refs_0_.3, ...), custom_call_target="tpu_custom_call" | custom-call | tf_op jit(solution)/shard_map/pallas_call | solution.py:1188
  334.9 5.3 %shard_map.336 = (f32[24,2304]{1,0:T(8,128)}, f32[24,768]{1,0:T(8,128)}, f32[24,3072]{1,0:T(8,128)}, f32[96,768]{1,0:T(8,128)}, bf16[3,512,768]{2,1,0:T(8,128)(2...) custom-call(f32[16,768]{1,0:T(8,128)} %get-tuple-element.78.sums, ...), custom_call_target="tpu_custom_call" | custom-call | tf_op jit(solution)/shard_map/pallas_call | solution.py:1256
where the time goes:
time: 343 us; the launch traced here: 340 us
  Pallas kernels  339 us (99%)
    pallas_call x1, Pallas kernels, forward_pass(): pl.pallas_call(forward_kernel, in_specs=[smem_spec(), smem_spec()] + [any...  140 us
    pallas_call x1, Pallas kernels, backward_pass(): pl.pallas_call(backward_kernel, grid=(GRAD_STEPS + PAIRS,), in_specs=[sme...  128 us
    pallas_call x1, Pallas kernels, student_middle(): pl.pallas_call(student_middle_kernel, grid=(rows, tokens // block), in_sp...  65.8 us

commit v1 on v0

--- a/solution.py
+++ b/solution.py
@@ -470,7 +470,7 @@
         barrier = pltpu.get_barrier_semaphore()
         for partner in partners:
             pl.semaphore_signal(barrier, inc=1, device_id=(partner,), device_id_type=MESH)
-        pl.semaphore_wait(barrier, len(partners))
+        return functools.partial(pl.semaphore_wait, barrier, len(partners))
 
 
 class Trip:
@@ -615,6 +615,15 @@
     return parts
 
 
+def choose(index, slots, stage):
+    if len(slots) == 1:
+        pl.when(index == slots[0])(functools.partial(stage, slots[0]))
+    elif slots:
+        low, high = slots[: len(slots) // 2], slots[len(slots) // 2 :]
+        pl.when(index < high[0])(functools.partial(choose, index, low, stage))
+        pl.when(index >= high[0])(functools.partial(choose, index, high, stage))
+
+
 def forward_kernel(*refs):
     lengths, clips = refs[:2]
     teacher_hbm, hidden_hbm = refs[2:4]
@@ -626,6 +635,7 @@
     send, receive, load, store = refs[46:]
     rows = t_x.shape[0]
     place = Place()
+    all_here = place.meet()
     inputs = [pltpu.make_async_copy(teacher_hbm, t_x, load.at[0]), pltpu.make_async_copy(hidden_hbm, a_in, load.at[1])]
     for copy in inputs:
         copy.start()
@@ -633,7 +643,7 @@
         for i in range(3):
             to, at = TRIPLE * pair + PAIR * i, D * i + PAIR * pair
             low[4][:, to : to + PAIR] = teach[0][:, at : at + PAIR]
-    place.meet()
+    all_here()
     sources = [low[4], *teach[1:], *low[:4]]
     parts = travel_parts([source.shape for source in sources])
     trips = [
@@ -685,8 +695,8 @@
                 do(at)
 
     def turn(first_slot, count, index):
-        for slot in sorted({when for when, _, _ in FORWARD_PLAN if first_slot <= when < first_slot + count}):
-            pl.when(index == slot - first_slot)(functools.partial(stage, slot))
+        planned = sorted({when for when, _, _ in FORWARD_PLAN if first_slot <= when < first_slot + count})
+        choose(index + first_slot, planned, stage)
 
     def await_parts(weight, pair, row):
         pairs_each = PAIRS // len(per[weight])
@@ -942,15 +952,15 @@
 FOLD_PARTS = sum(pieces for _, pieces in FOLDED)
 BACKWARD_PLAN = (
     (5, 0, 0), (5, 1, 0), (5, 2, 0), (5, 3, 0), (6, 4, 0), (7, 5, 0), (8, 6, 0), (9, 0, 1), (9, 7, 0), (9, 8,
-    0), (11, 1, 1), (12, 9, 0), (12, 0, 2), (12, 2, 1), (12, 15, 0), (14, 1, 2), (14, 3, 1), (14, 9, 1), (14,
-    15, 1), (15, 10, 0), (15, 0, 3), (15, 2, 2), (16, 15, 2), (17, 1, 3), (17, 4, 1), (17, 10, 1), (17, 9, 2),
-    (18, 11, 0), (18, 0, 4), (18, 2, 3), (18, 3, 2), (18, 15, 3), (19, 5, 1), (19, 1, 4), (19, 9, 3), (20, 10,
-    2), (20, 11, 1), (21, 12, 0), (21, 3, 3), (21, 4, 2), (21, 6, 1), (21, 15, 4), (22, 2, 4), (22, 5, 2), (22,
-    9, 4), (22, 10, 3), (22, 11, 2), (23, 12, 1), (24, 13, 0), (24, 3, 4), (24, 4, 3), (24, 7, 1), (24, 10, 4),
-    (24, 11, 3), (25, 5, 3), (25, 6, 2), (25, 12, 2), (26, 8, 1), (26, 13, 1), (27, 14, 0), (27, 7, 2), (27, 6,
-    3), (27, 11, 4), (27, 12, 3), (28, 4, 4), (29, 5, 4), (30, 8, 2), (30, 13, 2), (30, 14, 1), (30, 16, 0),
-    (30, 7, 3), (30, 12, 4), (30, 16, 1), (30, 6, 4), (30, 13, 3), (30, 7, 4), (30, 16, 2), (30, 8, 3), (30, 14,
-    2), (30, 13, 4), (30, 16, 3), (30, 14, 3), (30, 8, 4), (30, 16, 4), (30, 14, 4),
+    0), (11, 1, 1), (12, 9, 0), (12, 0, 2), (12, 2, 1), (12, 15, 0), (13, 1, 2), (14, 9, 1), (14, 15, 1), (15,
+    10, 0), (15, 0, 3), (15, 1, 3), (15, 2, 2), (15, 3, 1), (16, 9, 2), (16, 15, 2), (17, 10, 1), (18, 11, 0),
+    (18, 0, 4), (18, 1, 4), (18, 2, 3), (18, 3, 2), (18, 4, 1), (18, 9, 3), (18, 15, 3), (19, 10, 2), (20, 5,
+    1), (20, 11, 1), (21, 12, 0), (21, 2, 4), (21, 3, 3), (21, 4, 2), (21, 6, 1), (21, 9, 4), (21, 10, 3), (21,
+    15, 4), (22, 11, 2), (23, 5, 2), (23, 7, 1), (23, 12, 1), (24, 13, 0), (24, 3, 4), (24, 4, 3), (24, 6, 2),
+    (24, 10, 4), (24, 11, 3), (25, 8, 1), (26, 5, 3), (26, 12, 2), (26, 13, 1), (26, 7, 2), (27, 14, 0), (27, 4,
+    4), (27, 6, 3), (27, 8, 2), (27, 11, 4), (28, 12, 3), (29, 5, 4), (30, 7, 3), (30, 8, 3), (30, 13, 2), (30,
+    14, 1), (30, 16, 0), (30, 6, 4), (30, 12, 4), (30, 16, 1), (30, 13, 3), (30, 14, 2), (30, 16, 2), (30, 14,
+    3), (30, 16, 3), (30, 7, 4), (30, 8, 4), (30, 13, 4), (30, 16, 4), (30, 14, 4),
 )
 
 
@@ -1031,8 +1041,7 @@
                 act()
 
     def turn(index):
-        for slot in sorted({when for when, _ in timed if when < slots}):
-            pl.when(index == slot)(functools.partial(stage, slot))
+        choose(index, sorted({when for when, _ in timed if when < slots}), stage)
 
     def load_left(source):
         return pltpu.make_async_copy(source, x, load.at[2])
@@ -1057,12 +1066,13 @@
 
     @pl.when(at_step == 0)
     def _():
+        all_here = place.meet()
         load_left(d_down).start()
         load_chunk(0)
         inputs[1].start()
-        place.meet()
         q_sums[...] = jnp.zeros_like(q_sums)
         d_a[...] = jnp.zeros_like(d_a)
+        all_here()
 
     @pl.when(at_step < GRAD_STEPS)
     def _():
@@ -1224,14 +1234,20 @@
     outs, input_out = refs[5:9], refs[9]
     b_q, b_v, b_out, b_up, b_down, gain_one, shift_one, gain_two, shift_two, clips = refs[10:20]
     held, arrive = refs[20:]
-    copy = pltpu.make_async_copy(input_hbm, held, arrive)
-    copy.start()
+    rows = held.shape[0]
+    copies = [pltpu.make_async_copy(input_hbm.at[i], held.at[i], arrive.at[i]) for i in range(rows)]
+    for copy in copies:
+        copy.start()
 
     def row(ref, at):
         return ref[at : at + 1].reshape(D)
 
     for source, target in zip(grads, outs):
         target[...] = source[...]
+    backs = [pltpu.make_async_copy(held.at[i], input_out.at[i], arrive.at[rows + i]) for i in range(rows)]
+    for copy, back in zip(copies, backs):
+        copy.wait()
+        back.start()
     b_q[...] = row(q_sums, Q_QUERY)
     b_v[...] = row(q_sums, Q_VALUE)
     b_out[...] = row(sums, S_OUT)
@@ -1244,10 +1260,8 @@
     clips[0] = jnp.sum(q_sums[Q_CLIP : Q_CLIP + 1])
     for i, at in enumerate((S_CLIP_ONE, S_CLIP_TWO, S_CLIP_THREE)):
         clips[1 + i] = jnp.sum(sums[at : at + 1])
-    copy.wait()
-    back = pltpu.make_async_copy(held, input_out, arrive)
-    back.start()
-    back.wait()
+    for copy in backs:
+        copy.wait()
 
 
 def finish(sums, q_sums, grads, input_grad):
@@ -1261,7 +1275,7 @@
         + [shaped(input_grad.shape, BF16)]
         + [shaped((n,), F32) for n in lengths]
         + [shaped((4,), F32)],
-        scratch_shapes=[pltpu.VMEM(input_grad.shape, BF16), pltpu.SemaphoreType.DMA],
+        scratch_shapes=[pltpu.VMEM(input_grad.shape, BF16), pltpu.SemaphoreType.DMA((2 * input_grad.shape[0],))],
         compiler_params=params(),
     )(sums, q_sums, *grads, input_grad)
 

time: 343 us -> 338 us (0.985)
  Pallas kernels: 339 us -> 334 us
where the time goes in v1:
time: 338 us; the launch traced here: 335 us
  Pallas kernels  334 us (99%)
    pallas_call x1, Pallas kernels, forward_pass(): pl.pallas_call(forward_kernel, in_specs=[smem_spec(), smem_spec()] + [any...  138 us
    pallas_call x1, Pallas kernels, backward_pass(): pl.pallas_call(backward_kernel, grid=(GRAD_STEPS + PAIRS,), in_specs=[sme...  125 us
    pallas_call x1, Pallas kernels, student_middle(): pl.pallas_call(student_middle_kernel, grid=(rows, tokens // block), in_sp...  65.5 us

profile of v1, /device:TPU:0, one launch (start us, length us, event | category | flops | bytes accessed | tf_op | source)
XLA Modules:
  0.0 335.0 jit_solution(2657088293452557435)
XLA Ops:
  0.7 138.4 %shard_map.333 = (bf16[4,4,48,2304]{3,2,1,0:T(8,128)(2,1)}, bf16[4,4,48,768]{3,2,1,0:T(8,128)(2,1)}, bf16[4,4,48,3072]{3,2,1,0:T(8,128)(2,1)}, bf16[4,4,192,768]...) custom-call(s32[3]{0:T(128)} %refs_0_.3, ...), custom_call_target="tpu_custom_call" | custom-call | tf_op jit(solution)/shard_map/pallas_call | solution.py:781
  139.1 65.5 %shard_map.334 = (bf16[3,512,768]{2,1,0:T(8,128)(2,1)}, bf16[3,512,3072]{2,1,0:T(8,128)(2,1)}, bf16[3,512,3072]{2,1,0:T(8,128)(2,1)}, bf16[3,512,768]{2,1,0:T(8,...) custom-call(s32[3]{0:T(128)} %refs_0_.3, ...), custom_call_target="tpu_custom_call" | custom-call | tf_op jit(solution)/shard_map/pallas_call | solution.py:396
  204.6 125.4 %shard_map.335 = (bf16[3,512,768]{2,1,0:T(8,128)(2,1)}, bf16[4,4,2,96,768]{4,3,2,1,0:T(8,128)(2,1)}, bf16[4,4,2,24,3072]{4,3,2,1,0:T(8,128)(2,1)}, bf16[4,4,2,24...) custom-call(s32[3]{0:T(128)} %refs_0_.3, ...), custom_call_target="tpu_custom_call" | custom-call | tf_op jit(solution)/shard_map/pallas_call | solution.py:1198
  330.0 4.8 %shard_map.336 = (f32[24,2304]{1,0:T(8,128)}, f32[24,768]{1,0:T(8,128)}, f32[24,3072]{1,0:T(8,128)}, f32[96,768]{1,0:T(8,128)}, bf16[3,512,768]{2,1,0:T(8,128)(2...) custom-call(f32[16,768]{1,0:T(8,128)} %get-tuple-element.78.sums, ...), custom_call_target="tpu_custom_call" | custom-call | tf_op jit(solution)/shard_map/pallas_call | solution.py:1270

commit v2 on v1

--- a/solution.py
+++ b/solution.py
@@ -584,20 +584,19 @@
 
 
 T_QKV, T_OUT, T_UP, T_DOWN, B_QKV, B_OUT, B_UP, B_DOWN = range(8)
-TRAVEL = ((T_QKV, 6), (B_QKV, 2), (T_DOWN, 2), (T_OUT, 1), (T_UP, 2), (B_OUT, 1), (B_DOWN, 1), (B_UP, 2))
-EARLY = (T_OUT, B_OUT, B_UP,)
+TRAVEL = ((T_QKV, 6), (B_QKV, 2), (T_OUT, 1), (T_DOWN, 1), (T_UP, 2), (B_OUT, 1), (B_DOWN, 1), (B_UP, 2))
+EARLY = (T_UP, B_UP,)
 TALL = (T_DOWN, B_DOWN)
 FORWARD_PLAN = (
-    (0, 0, 0), (0, 1, 0), (0, 2, 0), (0, 3, 0), (0, 0, 1), (0, 4, 0), (0, 1, 1), (0, 5, 0), (0, 2, 1), (0, 6,
-    0), (0, 0, 2), (0, 3, 1), (0, 1, 2), (0, 4, 1), (0, 2, 2), (0, 5, 1), (0, 0, 3), (0, 7, 0), (0, 3, 2), (0,
-    6, 1), (0, 1, 3), (0, 0, 4), (0, 2, 3), (0, 4, 2), (0, 5, 2), (0, 8, 0), (0, 3, 3), (0, 1, 4), (1, 7, 1),
-    (2, 2, 4), (2, 3, 4), (2, 6, 2), (3, 4, 3), (3, 5, 3), (3, 9, 0), (4, 8, 1), (5, 4, 4), (5, 5, 4), (5, 7,
-    2), (6, 6, 3), (6, 10, 0), (8, 6, 4), (8, 9, 1), (8, 11, 0), (9, 10, 1), (10, 7, 3), (10, 8, 2), (13, 7, 4),
-    (13, 12, 0), (14, 9, 2), (14, 10, 2), (14, 8, 3), (14, 11, 1), (16, 13, 0), (17, 8, 4), (18, 12, 1), (18,
-    14, 0), (19, 13, 1), (19, 10, 3), (21, 10, 4), (23, 9, 3), (23, 11, 2), (24, 13, 2), (25, 12, 2), (25, 9,
-    4), (25, 15, 0), (27, 11, 3), (27, 14, 1), (28, 13, 3), (28, 15, 1), (29, 11, 4), (30, 12, 3), (30, 13, 4),
-    (31, 16, 0), (32, 12, 4), (33, 15, 2), (34, 16, 1), (36, 14, 2), (39, 15, 3), (39, 16, 2), (42, 14, 3), (42,
-    15, 4), (44, 16, 3), (45, 14, 4), (46, 16, 4),
+    (0, 0, 0), (0, 1, 0), (0, 2, 0), (0, 3, 0), (0, 4, 0), (0, 0, 1), (0, 5, 0), (0, 1, 1), (0, 6, 0), (0, 2,
+    1), (0, 3, 1), (0, 0, 2), (0, 4, 1), (0, 1, 2), (0, 5, 1), (0, 2, 2), (0, 3, 2), (0, 0, 3), (0, 7, 0), (0,
+    6, 1), (0, 4, 2), (0, 1, 3), (0, 0, 4), (0, 2, 3), (0, 3, 3), (0, 5, 2), (0, 8, 0), (0, 1, 4), (1, 4, 3),
+    (1, 7, 1), (1, 9, 0), (2, 2, 4), (2, 3, 4), (2, 5, 3), (2, 6, 2), (3, 4, 4), (3, 8, 1), (4, 5, 4), (6, 7,
+    2), (7, 10, 0), (8, 6, 3), (8, 8, 2), (9, 7, 3), (9, 9, 1), (9, 10, 1), (10, 6, 4), (11, 7, 4), (11, 8, 3),
+    (13, 8, 4), (13, 11, 0), (15, 10, 2), (16, 11, 1), (18, 9, 2), (19, 12, 0), (21, 10, 3), (21, 13, 0), (21,
+    11, 2), (23, 12, 1), (24, 9, 3), (24, 10, 4), (27, 9, 4), (27, 14, 0), (28, 11, 3), (28, 12, 2), (29, 13,
+    1), (29, 14, 1), (31, 11, 4), (31, 12, 3), (33, 12, 4), (33, 15, 0), (35, 14, 2), (36, 15, 1), (37, 13, 2),
+    (41, 14, 3), (41, 15, 2), (43, 13, 3), (44, 14, 4), (46, 13, 4), (46, 15, 3), (48, 15, 4),
 )
 
 

time: 338 us -> 335 us (level)
  no operation moved by 1% of the time
where the time goes in v2:
time: 335 us; the launch traced here: 333 us
  Pallas kernels  332 us (99%)
    pallas_call x1, Pallas kernels, forward_pass(): pl.pallas_call(forward_kernel, in_specs=[smem_spec(), smem_spec()] + [any...  136 us
    pallas_call x1, Pallas kernels, backward_pass(): pl.pallas_call(backward_kernel, grid=(GRAD_STEPS + PAIRS,), in_specs=[sme...  126 us
    pallas_call x1, Pallas kernels, student_middle(): pl.pallas_call(student_middle_kernel, grid=(rows, tokens // block), in_sp...  65.5 us

profile of v2, /device:TPU:0, one launch (start us, length us, event | category | flops | bytes accessed | tf_op | source)
XLA Modules:
  0.0 332.6 jit_solution(13175405937294537934)
XLA Ops:
  0.7 135.7 %shard_map.333 = (bf16[4,4,48,2304]{3,2,1,0:T(8,128)(2,1)}, bf16[4,4,48,768]{3,2,1,0:T(8,128)(2,1)}, bf16[4,4,48,3072]{3,2,1,0:T(8,128)(2,1)}, bf16[4,4,192,768]...) custom-call(s32[3]{0:T(128)} %refs_0_.3, ...), custom_call_target="tpu_custom_call" | custom-call | tf_op jit(solution)/shard_map/pallas_call | solution.py:780
  136.3 65.5 %shard_map.334 = (bf16[3,512,768]{2,1,0:T(8,128)(2,1)}, bf16[3,512,3072]{2,1,0:T(8,128)(2,1)}, bf16[3,512,3072]{2,1,0:T(8,128)(2,1)}, bf16[3,512,768]{2,1,0:T(8,...) custom-call(s32[3]{0:T(128)} %refs_0_.3, ...), custom_call_target="tpu_custom_call" | custom-call | tf_op jit(solution)/shard_map/pallas_call | solution.py:396
  201.9 125.8 %shard_map.335 = (bf16[3,512,768]{2,1,0:T(8,128)(2,1)}, bf16[4,4,2,96,768]{4,3,2,1,0:T(8,128)(2,1)}, bf16[4,4,2,24,3072]{4,3,2,1,0:T(8,128)(2,1)}, bf16[4,4,2,24...) custom-call(s32[3]{0:T(128)} %refs_0_.3, ...), custom_call_target="tpu_custom_call" | custom-call | tf_op jit(solution)/shard_map/pallas_call | solution.py:1197
  327.7 4.8 %shard_map.336 = (f32[24,2304]{1,0:T(8,128)}, f32[24,768]{1,0:T(8,128)}, f32[24,3072]{1,0:T(8,128)}, f32[96,768]{1,0:T(8,128)}, bf16[3,512,768]{2,1,0:T(8,128)(2...) custom-call(f32[16,768]{1,0:T(8,128)} %get-tuple-element.78.sums, ...), custom_call_target="tpu_custom_call" | custom-call | tf_op jit(solution)/shard_map/pallas_call | solution.py:1269
